TPU v7x, 32 devices: a whole 2x2x4 slice. The times are simulated.
32 devices in a mesh: grp: 2 (over x), seq: 8 (over z, y), tile: 2 (over core).
Axes of the slice: x: 2, y: 2, z: 4, core: 2. Of those that a mesh axis runs over, the one named last changes fastest.
Arguments:
- tiles: bfloat16 [16384, 1536], P(('grp', 'seq', 'tile')), parts along dimension 0, may hold values from -6 to 6
- producer: int32 [8192, 1], P('grp'), parts along dimension 0, may hold values from 0 to 15; in each aligned block of 256 rows (0 to 255, 256 to 511, ...) at most 32 rows name the same one
- slide_lengths: int32 [8], P('grp'), parts along dimension 0, may hold values from 1 to 2048, 4096 in all
- dilation: int32 [4], replicated, may hold values from 1 to 8, as said below
- in_weight: bfloat16 [1536, 768], replicated, may hold values from -0.15625 to 0.15625
- in_bias: float32 [768], replicated, may hold values from -3 to 3
- norm_gain: float32 [768], replicated, may hold values from 0.1 to 1.9
- norm_bias: float32 [768], replicated, may hold values from -3 to 3
- qkv_weight: bfloat16 [3, 768, 768], P(None, None, 'tile'), may hold values from -1.5 to 1.5
- qkv_bias: float32 [3, 768], P(None, 'tile'), may hold values from -3 to 3
- out_weight: bfloat16 [768, 768], P('tile'), may hold values from -0.21875 to 0.21875
- out_bias: float32 [768], replicated, may hold values from -3 to 3
Outputs:
- embedded: bfloat16 [8192, 768], P(('grp', 'seq', 'tile')), parts along dimension 0
- branch: bfloat16 [8192, 768], P(('grp', 'seq', 'tile')), parts along dimension 0
There are 2 independent parts, one for each index of `grp`. A program takes and returns all parts, laid end to end along the dimension named above; an argument that names none is the same for every part. Nothing has to cross between parts.
Inputs may be any that keep to these rules, and one draw needn't show every extreme that they name: In each aligned block of 256 positions no producer appears more than 32 times; in every draw some producer appears exactly 32 times in some block, and every producer appears somewhere. `slide_lengths`: the lengths sum to 4096; the largest is exactly 2048. Every entry is a power of two; in every draw some group has dilation 1 and some group has 8.
All inputs are finite; a program needn't handle non-finite values.
Results may differ from a plain program's by a relative error of at most 0.011.
Values may be sent and summed in bfloat16 or wider, within the bound.
A program may use at most 64 MiB of HBM per device.

v0:
```python
import math

import jax
import jax.numpy as jnp
from jax import lax
from jax.sharding import PartitionSpec as P

HEADS = 16


def swapped(block, axis, stride):
    count = lax.axis_size(axis)
    route = []
    for low in range(count):
        high = low | 1 << stride
        if high != low and high < count:
            route += [(low, high), (high, low)]
    return lax.ppermute(block, axis, route)


def project_rows(source_rows, in_weight, in_bias):
    summed = jnp.dot(source_rows, in_weight, preferred_element_type=jnp.float32) + in_bias
    return summed.astype(jnp.bfloat16)


def split_halves(blocks, bit_index, seq_index):
    total_rows, row_width = blocks.shape
    spacing = 1 << bit_index
    halves = blocks.reshape(total_rows // (2 * spacing), 2, spacing, row_width)
    keeps_low = jnp.bitwise_and(jnp.right_shift(seq_index, bit_index), 1) == 0
    leaving = jnp.where(keeps_low, halves[:, 1], halves[:, 0])
    return (halves, keeps_low, leaving)


def join_halves(blocks, halves, keeps_low, incoming, active):
    lower = jnp.where(keeps_low, halves[:, 0], incoming)
    upper = jnp.where(keeps_low, incoming, halves[:, 1])
    joined = jnp.stack([lower, upper], axis=1).reshape(blocks.shape)
    return jnp.where(active[None, :], joined, blocks)


def segment_attention(queries, key_rows, values, slide_ids, score_scale):
    scores = (
        jnp.einsum("qhd,khd->hqk", queries, key_rows, preferred_element_type=jnp.float32)
        * score_scale
    )
    allowed = slide_ids[:, None] == slide_ids[None, :]
    scores = jnp.where(allowed[None], scores, -1e30)
    row_peak = jnp.max(scores, axis=2, keepdims=True)
    exponent = jnp.where(allowed[None], jnp.exp(scores - row_peak), 0.0)
    weights = (exponent / jnp.sum(exponent, axis=2, keepdims=True)).astype(jnp.bfloat16)
    mixed_rows = jnp.einsum("hqk,khd->qhd", weights, values, preferred_element_type=jnp.float32)
    return mixed_rows.astype(jnp.bfloat16)


def on_device(
    tiles,
    producer,
    slide_lengths,
    dilation,
    in_weight,
    in_bias,
    norm_gain,
    norm_bias,
    qkv_weight,
    qkv_bias,
    out_weight,
    out_bias,
):
    seq_count = lax.axis_size("seq")
    tile_count = lax.axis_size("tile")
    seq_index = lax.axis_index("seq")
    tile_index = lax.axis_index("tile")
    devices = seq_count * tile_count
    own_rank = seq_index * tile_count + tile_index
    capacity = tiles.shape[0]
    window = producer.shape[0]
    dest_rows = window // devices
    per_pair = capacity // devices
    owners = producer[:, 0].reshape(devices, dest_rows)
    counts = jnp.sum((owners == own_rank).astype(jnp.int32), axis=1)
    starts = jnp.cumsum(counts) - counts
    slot_ids = jnp.arange(per_pair, dtype=jnp.int32)
    is_live = slot_ids[None, :] < counts[:, None]
    pick_rows = jnp.where(is_live, starts[:, None] + slot_ids[None, :], 0).reshape(-1)
    source = project_rows(tiles, in_weight, in_bias)
    outgoing = jnp.where(
        is_live.reshape(-1)[:, None],
        jnp.take(source, pick_rows, axis=0),
        jnp.zeros((), source.dtype),
    )
    arrived = lax.all_to_all(outgoing, ("seq", "tile"), split_axis=0, concat_axis=0, tiled=True)
    own_owners = lax.dynamic_index_in_dim(owners, own_rank, 0, keepdims=False)
    onehot = (own_owners[:, None] == jnp.arange(devices, dtype=jnp.int32)[None, :]).astype(
        jnp.int32
    )
    arrival_rank = jnp.sum((jnp.cumsum(onehot, axis=0) - 1) * onehot, axis=1)
    placed = jnp.take(arrived, own_owners * per_pair + arrival_rank, axis=0)
    widened = placed.astype(jnp.float32)
    center = widened - jnp.mean(widened, axis=1, keepdims=True)
    spread = jnp.mean(center * center, axis=1, keepdims=True)
    normed = (center * lax.rsqrt(spread + 1e-05) * norm_gain + norm_bias).astype(jnp.bfloat16)
    local_groups = dilation.shape[0] // tile_count
    local_cols = qkv_weight.shape[2]
    group_cols = local_cols // local_groups
    weight_pieces = []
    bias_pieces = []
    for group_id in range(local_groups):
        for member_id in range(3):
            weight_pieces.append(
                qkv_weight[member_id, :, group_id * group_cols : (group_id + 1) * group_cols]
            )
            bias_pieces.append(
                qkv_bias[member_id, group_id * group_cols : (group_id + 1) * group_cols]
            )
    joined_weight = jnp.concatenate(weight_pieces, axis=1)
    joined_bias = jnp.concatenate(bias_pieces)
    projected = (
        jnp.dot(
            lax.all_gather(normed, "tile", axis=0, tiled=True),
            joined_weight,
            preferred_element_type=jnp.float32,
        )
        + joined_bias
    ).astype(jnp.bfloat16)
    total_rows = projected.shape[0]
    largest = min(16, seq_count)
    levels = largest.bit_length() - 1
    own_dilations = lax.dynamic_slice_in_dim(dilation, tile_index * local_groups, local_groups)
    regrouped = projected
    for bit_index in range(levels):
        halves, keeps_low, leaving = split_halves(regrouped, bit_index, seq_index)
        incoming = swapped(leaving, "seq", bit_index)
        active = jnp.repeat(1 << bit_index < own_dilations, 3 * group_cols)
        regrouped = join_halves(regrouped, halves, keeps_low, incoming, active)
    head_dim = in_weight.shape[1] // HEADS
    heads_here = group_cols // head_dim
    score_scale = 1.0 / math.sqrt(head_dim)
    row_ids = jnp.arange(total_rows, dtype=jnp.int32)
    slide_ends = jnp.cumsum(slide_lengths)
    outputs = []
    for group_id in range(local_groups):
        low_mask = own_dilations[group_id] - 1
        source_shard = (
            seq_index - jnp.bitwise_and(seq_index, low_mask) + jnp.bitwise_and(row_ids, low_mask)
        )
        true_row = (
            row_ids - jnp.bitwise_and(row_ids, low_mask) + jnp.bitwise_and(seq_index, low_mask)
        )
        positions = source_shard * total_rows + true_row
        slide_ids = jnp.sum((positions[:, None] >= slide_ends[None, :]).astype(jnp.int32), axis=1)
        first = group_id * 3 * group_cols
        queries = regrouped[:, first : first + group_cols].reshape(total_rows, heads_here, head_dim)
        key_rows = regrouped[:, first + group_cols : first + 2 * group_cols].reshape(
            total_rows, heads_here, head_dim
        )
        values = regrouped[:, first + 2 * group_cols : first + 3 * group_cols].reshape(
            total_rows, heads_here, head_dim
        )
        outputs.append(
            segment_attention(queries, key_rows, values, slide_ids, score_scale).reshape(
                total_rows, group_cols
            )
        )
    attended = jnp.concatenate(outputs, axis=1)
    for bit_index in reversed(range(levels)):
        halves, keeps_low, leaving = split_halves(attended, bit_index, seq_index)
        incoming = swapped(leaving, "seq", bit_index)
        active = jnp.repeat(1 << bit_index < own_dilations, group_cols)
        attended = join_halves(attended, halves, keeps_low, incoming, active)
    summed = lax.psum_scatter(
        jnp.dot(attended, out_weight, preferred_element_type=jnp.float32).astype(jnp.bfloat16),
        "tile",
        scatter_dimension=0,
        tiled=True,
    ).astype(jnp.float32)
    branch = (summed + out_bias).astype(jnp.bfloat16)
    return (placed, branch)


def solution(mesh):
    return jax.shard_map(
        on_device,
        mesh=mesh,
        in_specs=(
            P(("grp", "seq", "tile"), None),
            P("grp", None),
            P("grp"),
            P(),
            P(),
            P(),
            P(),
            P(),
            P(None, None, "tile"),
            P(None, "tile"),
            P("tile", None),
            P(),
        ),
        out_specs=(P(("grp", "seq", "tile"), None), P(("grp", "seq", "tile"), None)),
        check_vma=False,
    )
```

profile of v0, /device:TPU:0, one launch (start us, length us, event | category | flops | bytes accessed | tf_op | source)
XLA Modules:
  0.0 183.7 jit_solution(8534680662082661242)
XLA Ops:
  7.7 1.6 reduce.6
  9.9 2.8 %add_convert_fusion = bf16[512,768]{1,0:T(8,128)(2,1)S(1)} fusion(bf16[512,1536]{1,0:T(8,128)(2,1)} %param.12, bf16[1536,768]{1,0:T(8,128)(2,1)S(1)} %copy-done, f32[768]{0:T(1024)} %param.17), kind=kOutput, calls=%fused_computation.22 | convolution fusion | flops 1208745984 | bytes 4721664 | tf_op jit(solution)/shard_map/dot_general | solution.py:22
  12.7 2.0 %gather_fusion = bf16[512,768]{1,0:T(8,128)(2,1)S(1)} fusion(bf16[512,768]{1,0:T(8,128)(2,1)S(1)} %add_convert_fusion, s32[1024]{0:T(1024)S(1)} %pad_clamp_fusion.1), kind=kCustom, calls=%fused_computation | custom fusion | bytes 1574912 | tf_op jit(solution)/shard_map/jit(_take)/gather | solution.py:89
  14.8 1.1 select_select_fusion
  15.9 7.4 %all-to-all-start = ((bf16[16,32,768]{2,1,0:T(8,128)(2,1)}), bf16[16,32,768]{2,1,0:T(8,128)(2,1)S(1)}, u32[]{:S(2)}, u32[]{:S(2)}) async-start(bf16[16,32,768]{2,1,0:T(8,128)(2,1)} %select_select_fusion), calls=%async_computation | async-start | bytes 1572864 | tf_op jit(solution)/shard_map/all_to_all | solution.py:92
  24.3 1.6 slice_bitcast_fusion.4
  25.9 4.1 %concatenate.36 = bf16[768,1152]{1,0:T(8,128)(2,1)} concatenate(bf16[768,192]{1,0:T(8,128)(2,1)} %get-tuple-element.16, bf16[768,192]{1,0:T(8,128)(2,1)} %get-tuple-element.15, bf16[768,192]{1,0:T(8,128)(2,1)} %get-tuple-element.14, bf16[768,192]{1,0:T(8,128)(2,1)S(1)} %get-tuple-element.13, bf16[768,192]{1,0:T(8,128)(2,1)} %get-tuple-element.17, ...), dimensions={1} | concatenate | bytes 3538944 | tf_op jit(solution)/shard_map/concatenate | solution.py:116
  30.1 11.8 %all-to-all-done = bf16[16,32,768]{2,1,0:T(8,128)(2,1)S(1)} async-done(((bf16[16,32,768]{2,1,0:T(8,128)(2,1)}), bf16[16,32,768]{2,1,0:T(8,128)(2,1)S(1)}, u32[]{:S(2)}, u32[]{:S(2)}) %all-to-all-start) | async-done | bytes 786464 | tf_op jit(solution)/shard_map/all_to_all | solution.py:92
  42.0 1.2 gather_fusion.1
  44.2 2.5 %all_gather.3 = bf16[512,768]{1,0:T(8,128)(2,1)S(1)} all-gather(bf16[256,768]{1,0:T(8,128)(2,1)S(1)} %fusion.20), channel_id=1, replica_groups=mesh['grp'=2,'seq'=8,'tile'=2] {'tile'}, dimensions={0}, use_global_device_ids=true | all-gather | bytes 1179648 | tf_op jit(solution)/shard_map/all_gather | solution.py:120
  46.7 1.2 fusion.4
  49.4 1.6 fusion.48
  51.2 1.6 collective-permute-start
  54.1 12.7 %collective-permute-done = bf16[256,1,1152]{2,0,1:T(8,128)(2,1)S(1)} collective-permute-done((bf16[256,1,1152]{2,0,1:T(8,128)(2,1)S(1)}, bf16[256,1,1152]{2,0,1:T(8,128)(2,1)S(1)}, u32[]{:S(2)}, u32[]{:S(2)}) %collective-permute-start) | collective-permute-done | bytes 589856 | tf_op jit(solution)/shard_map/ppermute | solution.py:18
  67.1 1.2 copy.120
  70.9 2.7 %collective-permute-start.1 = (bf16[128,2,1152]{2,1,0:T(2,128)(2,1)S(1)}, bf16[128,2,1152]{2,1,0:T(2,128)(2,1)S(1)}, u32[]{:S(2)}, u32[]{:S(2)}) collective-permute-start(bf16[128,2,1152]{2,1,0:T(2,128)(2,1)S(1)} %broadcast_select_fusion.3), channel_id=1, source_target_pairs={{0,4},{4,0},{2,6},{6,2},{8,12},{12,8},{10,14},{14,10},{1,5},{5,1},... | collective-permute-start | bytes 1769480 | tf_op jit(solution)/shard_map/ppermute | solution.py:18
  73.8 12.9 %collective-permute-done.1 = bf16[128,2,1152]{2,1,0:T(2,128)(2,1)S(1)} collective-permute-done((bf16[128,2,1152]{2,1,0:T(2,128)(2,1)S(1)}, bf16[128,2,1152]{2,1,0:T(2,128)(2,1)S(1)}, u32[]{:S(2)}, u32[]{:S(2)}) %collective-permute-start.1) | collective-permute-done | bytes 589856 | tf_op jit(solution)/shard_map/ppermute | solution.py:18
  87.7 1.5 pad_maximum_fusion.1
  90.5 2.4 %collective-permute-start.2 = (bf16[64,4,1152]{2,1,0:T(4,128)(2,1)S(1)}, bf16[64,4,1152]{2,1,0:T(4,128)(2,1)S(1)}, u32[]{:S(2)}, u32[]{:S(2)}) collective-permute-start(bf16[64,4,1152]{2,1,0:T(4,128)(2,1)S(1)} %broadcast_select_fusion.9), channel_id=1, source_target_pairs={{0,8},{8,0},{2,10},{10,2},{4,12},{12,4},{6,14},{14,6},{1,9},{9,1},... | collective-permute-start | bytes 1769480 | tf_op jit(solution)/shard_map/ppermute | solution.py:18
  95.3 1.2 broadcast_compare_fusion
  96.5 21.8 %collective-permute-done.2 = bf16[64,4,1152]{2,1,0:T(4,128)(2,1)S(1)} collective-permute-done((bf16[64,4,1152]{2,1,0:T(4,128)(2,1)S(1)}, bf16[64,4,1152]{2,1,0:T(4,128)(2,1)S(1)}, u32[]{:S(2)}, u32[]{:S(2)}) %collective-permute-start.2) | collective-permute-done | bytes 589856 | tf_op jit(solution)/shard_map/ppermute | solution.py:18
  121.6 3.9 %fusion.53 = (f32[4,512]{1,0:T(4,128)S(1)}, f32[4,512,512]{1,2,0:T(8,128)}) fusion(pred[512,512]{0,1:T(8,128)(4,1)S(1)} %copy-done.8, bf16[512,4,48]{0,2,1:T(8,128)(2,1)S(1)} %bitcast.200, bf16[512,4,48]{0,2,1:T(8,128)(2,1)S(1)} %bitcast.199), kind=kOutput, calls=%fused_computation.144 | convolution fusion | flops 105906688 | bytes 4857856 | tf_op jit(solution)/shard_map/sub | solution.py:50
  125.6 2.7 %fusion.14 = bf16[4,48,512]{2,1,0:T(8,128)(2,1)S(1)} fusion(bf16[512,4,48]{0,2,1:T(8,128)(2,1)S(1)} %bitcast.201, f32[4,512,512]{1,2,0:T(8,128)} %get-tuple-element.51, f32[4,512]{1,0:T(4,128)S(1)} %get-tuple-element.50), kind=kOutput, calls=%fused_computation.34 | convolution fusion | flops 102858752 | bytes 4595712 | tf_op jit(solution)/shard_map/hqk,khd->qhd/dot_general | solution.py:52
  128.9 4.0 %fusion.52 = (f32[4,512]{1,0:T(4,128)S(1)}, f32[4,512,512]{1,2,0:T(8,128)}) fusion(pred[512,512]{0,1:T(8,128)(4,1)S(1)} %copy-done.7, bf16[512,4,48]{0,2,1:T(8,128)(2,1)S(1)} %bitcast.198, bf16[512,4,48]{0,2,1:T(8,128)(2,1)S(1)} %bitcast.196), kind=kOutput, calls=%fused_computation.143 | convolution fusion | flops 105906688 | bytes 4857856 | tf_op jit(solution)/shard_map/sub | solution.py:50
  132.9 2.7 %fusion.13 = bf16[4,48,512]{2,1,0:T(8,128)(2,1)S(1)} fusion(bf16[512,4,48]{0,2,1:T(8,128)(2,1)S(1)} %bitcast.197, f32[4,512,512]{1,2,0:T(8,128)} %get-tuple-element.49, f32[4,512]{1,0:T(4,128)S(1)} %get-tuple-element.48), kind=kOutput, calls=%fused_computation.33 | convolution fusion | flops 102858752 | bytes 4595712 | tf_op jit(solution)/shard_map/hqk,khd->qhd/dot_general | solution.py:52
  138.0 9.7 %collective-permute-done.3 = bf16[64,4,384]{2,1,0:T(4,128)(2,1)S(1)} collective-permute-done((bf16[64,4,384]{2,1,0:T(4,128)(2,1)S(1)}, bf16[64,4,384]{2,1,0:T(4,128)(2,1)S(1)}, u32[]{:S(2)}, u32[]{:S(2)}) %collective-permute-start.3) | collective-permute-done | bytes 196640 | tf_op jit(solution)/shard_map/ppermute | solution.py:18
  150.7 5.3 %collective-permute-done.4 = bf16[128,2,384]{2,0,1:T(8,128)(2,1)S(1)} collective-permute-done((bf16[128,2,384]{2,0,1:T(8,128)(2,1)S(1)}, bf16[128,2,384]{2,0,1:T(8,128)(2,1)S(1)}, u32[]{:S(2)}, u32[]{:S(2)}) %collective-permute-start.4) | collective-permute-done | bytes 196640 | tf_op jit(solution)/shard_map/ppermute | solution.py:18
  156.6 1.3 broadcast_select_fusion.7
  161.6 3.0 %collective-permute-done.5 = bf16[256,1,384]{2,0,1:T(8,128)(2,1)S(1)} collective-permute-done((bf16[256,1,384]{2,0,1:T(8,128)(2,1)S(1)}, bf16[256,1,384]{2,0,1:T(8,128)(2,1)S(1)}, u32[]{:S(2)}, u32[]{:S(2)}) %collective-permute-start.5) | collective-permute-done | bytes 196640 | tf_op jit(solution)/shard_map/ppermute | solution.py:18
  165.3 3.0 %convolution_convert_fusion = bf16[512,768]{1,0:T(8,128)(2,1)} fusion(bf16[384,768]{1,0:T(8,128)(2,1)} %param.22, bf16[512,384]{1,0:T(8,128)(2,1)S(1)} %reshape.498, bf16[512,384]{1,0:T(8,128)(2,1)S(1)} %reshape.499, bf16[512,384]{1,0:T(8,128)(2,1)S(1)} %reshape.500, bf16[512,192]{1,0:T(8,128)(2,1)} %copy.153, bf16[512,192]{1,0:T(8,128)(2,1)} %copy.152, ...), kind=kOutput, calls=%fused_computation.23 | convolution fusion | flops 303759360 | bytes 2950272 | tf_op jit(solution)/shard_map/dot_general | solution.py:172
  168.3 6.8 %reduce-scatter.2.cloned.1.call-done = bf16[256,768]{1,0:T(8,128)(2,1)} async-done(((bf16[512,768]{1,0:T(8,128)(2,1)}), bf16[256,768]{1,0:T(8,128)(2,1)}) %reduce-scatter.2.cloned.1.call-update) | async-done | bytes 393232 | tf_op jit(solution)/shard_map/reduce_scatter | solution.py:171
  175.1 1.8 add_convert_fusion.1
  (152 shorter events, 26.5 us)
Async XLA Ops:
  7.2 2.8 %copy-start = (bf16[1536,768]{1,0:T(8,128)(2,1)S(1)}, bf16[1536,768]{1,0:T(8,128)(2,1)}, u32[]{:S(2)}) copy-start(bf16[1536,768]{1,0:T(8,128)(2,1)} %param.16) | copy-start | bytes 7077892
  14.8 9.4 %copy-start.9 = (f32[3,384]{1,0:T(4,128)S(1)}, f32[3,384]{1,0:T(4,128)}, u32[]{:S(2)}) copy-start(f32[3,384]{1,0:T(4,128)} %param.21) | copy-start | bytes 13828
  14.8 9.5 %copy-start.5 = (bf16[3,768,384]{2,1,0:T(8,128)(2,1)S(1)}, bf16[3,768,384]{2,1,0:T(8,128)(2,1)}, u32[]{:S(2)}) copy-start(bf16[3,768,384]{2,1,0:T(8,128)(2,1)} %param.20) | copy-start | bytes 5308420
  15.9 26.1 %all-to-all-start = ((bf16[16,32,768]{2,1,0:T(8,128)(2,1)}), bf16[16,32,768]{2,1,0:T(8,128)(2,1)S(1)}, u32[]{:S(2)}, u32[]{:S(2)}) async-start(bf16[16,32,768]{2,1,0:T(8,128)(2,1)} %select_select_fusion), calls=%async_computation | async-start | bytes 1572864 | tf_op jit(solution)/shard_map/all_to_all | solution.py:92
  23.3 151.8 %reduce-scatter.2.cloned.1.call-start = ((), (), s32[]{:S(2)}) async-start(), calls=%async_computation.2 | async-start | bytes 1179648 | tf_op jit(solution)/shard_map/reduce_scatter | solution.py:171
  24.2 1.8 copy-start.10
  25.9 4.1 %slice-start = ((s32[16,3]{0,1:T(4,128)}), s32[16,2]{0,1:T(2,128)S(1)}, s32[]{:S(2)}) async-start(s32[16,3]{0,1:T(4,128)} %copy-done.10), calls=%async_computation.3 | async-start | bytes 2048 | tf_op jit(solution)/shard_map/slice.1
  42.0 1.7 copy-start.11
  42.0 1.7 copy-start.12
  43.2 3.5 %copy-start.6 = (bf16[768,1152]{1,0:T(8,128)(2,1)S(1)}, bf16[768,1152]{1,0:T(8,128)(2,1)}, u32[]{:S(2)}) copy-start(bf16[768,1152]{1,0:T(8,128)(2,1)} %concatenate.36) | copy-start | bytes 5308420
  43.4 0.8 copy-start.4
  47.9 1.0 copy-start.2
  51.0 1.8 copy-start.14
  51.2 15.6 %collective-permute-start = (bf16[256,1,1152]{2,0,1:T(8,128)(2,1)S(1)}, bf16[256,1,1152]{2,0,1:T(8,128)(2,1)S(1)}, u32[]{:S(2)}, u32[]{:S(2)}) collective-permute-start(bf16[256,1,1152]{2,0,1:T(8,128)(2,1)S(1)} %broadcast_select_fusion.8), channel_id=1, source_target_pairs={{0,2},{2,0},{4,6},{6,4},{8,10},{10,8},{12,14},{14,12},{1,3},{3,1},... | collective-permute-start | bytes 1769480 | tf_op jit(solution)/shard_map/ppermute | solution.py:18
  53.4 0.5 copy-start.15
  68.3 1.3 copy-start.3
  69.7 3.9 %copy-start.17 = (pred[2]{0:T(512)(128)(4,1)S(1)}, pred[2]{0:T(512)(128)(4,1)}, u32[]{:S(2)}) copy-start(pred[2]{0:T(512)(128)(4,1)} %get-tuple-element.45) | copy-start | bytes 10
  70.9 15.8 %collective-permute-start.1 = (bf16[128,2,1152]{2,1,0:T(2,128)(2,1)S(1)}, bf16[128,2,1152]{2,1,0:T(2,128)(2,1)S(1)}, u32[]{:S(2)}, u32[]{:S(2)}) collective-permute-start(bf16[128,2,1152]{2,1,0:T(2,128)(2,1)S(1)} %broadcast_select_fusion.3), channel_id=1, source_target_pairs={{0,4},{4,0},{2,6},{6,2},{8,12},{12,8},{10,14},{14,10},{1,5},{5,1},... | collective-permute-start | bytes 1769480 | tf_op jit(solution)/shard_map/ppermute | solution.py:18
  89.9 3.7 %copy-start.19 = (s32[4]{0:T(128)S(1)}, s32[4]{0:T(128)}, u32[]{:S(2)}) copy-start(s32[4]{0:T(128)} %param.14) | copy-start | bytes 52
  90.5 27.8 %collective-permute-start.2 = (bf16[64,4,1152]{2,1,0:T(4,128)(2,1)S(1)}, bf16[64,4,1152]{2,1,0:T(4,128)(2,1)S(1)}, u32[]{:S(2)}, u32[]{:S(2)}) collective-permute-start(bf16[64,4,1152]{2,1,0:T(4,128)(2,1)S(1)} %broadcast_select_fusion.9), channel_id=1, source_target_pairs={{0,8},{8,0},{2,10},{10,2},{4,12},{12,4},{6,14},{14,6},{1,9},{9,1},... | collective-permute-start | bytes 1769480 | tf_op jit(solution)/shard_map/ppermute | solution.py:18
  120.7 1.0 copy-start.8
  125.5 3.4 %copy-start.7 = (pred[512,512]{0,1:T(8,128)(4,1)S(1)}, pred[512,512]{0,1:T(8,128)(4,1)}, u32[]{:S(2)}) copy-start(pred[512,512]{0,1:T(8,128)(4,1)} %get-tuple-element.52) | copy-start | bytes 786436
  136.7 11.0 %collective-permute-start.3 = (bf16[64,4,384]{2,1,0:T(4,128)(2,1)S(1)}, bf16[64,4,384]{2,1,0:T(4,128)(2,1)S(1)}, u32[]{:S(2)}, u32[]{:S(2)}) collective-permute-start(bf16[64,4,384]{2,1,0:T(4,128)(2,1)S(1)} %broadcast_select_fusion.11), channel_id=1, source_target_pairs={{0,8},{8,0},{2,10},{10,2},{4,12},{12,4},{6,14},{14,6},{1,9},{9,1},... | collective-permute-start | bytes 589832 | tf_op jit(solution)/shard_map/ppermute | solution.py:18
  148.3 0.9 copy-start.18
  149.2 6.9 %collective-permute-start.4 = (bf16[128,2,384]{2,0,1:T(8,128)(2,1)S(1)}, bf16[128,2,384]{2,0,1:T(8,128)(2,1)S(1)}, u32[]{:S(2)}, u32[]{:S(2)}) collective-permute-start(bf16[128,2,384]{2,0,1:T(8,128)(2,1)S(1)} %broadcast_select_fusion.12), channel_id=1, source_target_pairs={{0,4},{4,0},{2,6},{6,2},{8,12},{12,8},{10,14},{14,10},{1,5},{5,1},... | collective-permute-start | bytes 589832 | tf_op jit(solution)/shard_map/ppermute | solution.py:18
  157.9 1.6 copy-start.16
  158.5 6.0 %collective-permute-start.5 = (bf16[256,1,384]{2,0,1:T(8,128)(2,1)S(1)}, bf16[256,1,384]{2,0,1:T(8,128)(2,1)S(1)}, u32[]{:S(2)}, u32[]{:S(2)}) collective-permute-start(bf16[256,1,384]{2,0,1:T(8,128)(2,1)S(1)} %bitcast_select_fusion.1), channel_id=1, source_target_pairs={{0,2},{2,0},{4,6},{6,4},{8,10},{10,8},{12,14},{14,12},{1,3},{3,1},... | collective-permute-start | bytes 589832 | tf_op jit(solution)/shard_map/ppermute | solution.py:18
  165.3 9.8 %copy-start.13 = (f32[768]{0:T(1024)S(1)}, f32[768]{0:T(1024)}, u32[]{:S(2)}) copy-start(f32[768]{0:T(1024)} %param.23) | copy-start | bytes 9220
  165.3 11.6 %copy-start.1 = (bf16[1536,768]{1,0:T(8,128)(2,1)S(1)}, bf16[1536,768]{1,0:T(8,128)(2,1)}, u32[]{:S(2)}) copy-start(bf16[1536,768]{1,0:T(8,128)(2,1)} %param.16) | copy-start | bytes 7077892
Sparse Core Ops, SparseCore 0:
  168.4 6.6 reduce-scatter.1
where the time goes:
time: 184 us
  waiting for transfers between devices  84 us (46%)
  local copies, waits for them, and re-layouts  28.6 us (16%)
  matrix products  20.2 us (11%)
  other arithmetic  17 us (9%)
  between operations  16.1 us (9%)
  starting transfers between devices  15.2 us (8%)
  blocking collectives  2.54 us (1%)
    ppermute x6, waiting for transfers between devices, swapped(): return lax.ppermute(block, axis, route)  65.4 us
    all_to_all x1, waiting for transfers between devices, on_device(): lax.all_to_all(outgoing, ('seq', 'tile'), split_axis=0, concat_axis=0, ti...  11.8 us
    sub x2, matrix products, segment_attention(): exponent = jnp.where(allowed[None], jnp.exp(scores - row_peak), 0.0)  7.9 us
    ppermute x6, starting transfers between devices, swapped(): return lax.ppermute(block, axis, route)  7.82 us
    all_to_all x1, starting transfers between devices, on_device(): lax.all_to_all(outgoing, ('seq', 'tile'), split_axis=0, concat_axis=0, ti...  7.39 us
    reduce_scatter x1, waiting for transfers between devices, on_device(): lax.psum_scatter(jnp.dot(attended, out_weight, preferred_element_type=jnp...  6.8 us
    dot_general x2, matrix products, segment_attention(): jnp.einsum('hqk,khd->qhd', weights, values, preferred_element_type=jnp.fl...  5.38 us
    another operation x12, other arithmetic, join_halves(): joined = jnp.stack([lower, upper], axis=1).reshape(blocks.shape)  5.01 us
  transfers between devices with their start and end apart: 8, of which 8 were waited for; matrix products, arithmetic and copies ran while one was open for 8% of the time, Pallas kernels for 0%

commit v1 on v0

v1 whole, which is shorter than its diff:
```python
import functools
import math

import jax
import jax.numpy as jnp
from jax import lax
from jax.experimental import pallas as pl
from jax.experimental.pallas import tpu as pltpu
from jax.sharding import PartitionSpec as P

HEADS = 16
MESH = pl.DeviceIdType.MESH
BF = jnp.bfloat16
F32 = jnp.float32
VMEM_CAP = 56 * 1024 * 1024


def bit_of(value, bit):
    return (value // (1 << bit)) % 2


def reversed_bits(value, bits):
    total = 0
    for bit in range(bits):
        total = total + bit_of(value, bit) * (1 << (bits - 1 - bit))
    return total


def partner(seq, bit, low):
    span = 1 << bit
    return (seq // (2 * span)) * (2 * span) + (1 - bit_of(seq, bit)) * span + low


def exact_dot(a, b):
    return jnp.dot(a, b, preferred_element_type=F32)


def exchange_plan(levels):
    return [(bit, turn) for bit in reversed(range(levels)) for turn in range(1 << bit)]


def hand_over(
    levels, tiles, weight, bias, pick, own, gain, shift, placed, rows, outbox, inbox,
    send_a, recv_a, send_b, recv_b, send_c, recv_c,
):
    seq_n, tile_n = lax.axis_size("seq"), lax.axis_size("tile")
    devices = seq_n * tile_n
    seq, core = lax.axis_index("seq"), lax.axis_index("tile")
    other = 1 - core
    me = seq * tile_n + core
    per_pair = outbox.shape[1]
    block = own.shape[0]
    width = outbox.shape[2]
    barrier = pltpu.get_barrier_semaphore()
    for k in range(1, devices):
        peer = (me + k) % devices
        pl.semaphore_signal(
            barrier, inc=1, device_id={"seq": peer // tile_n, "tile": peer % tile_n}, device_id_type=MESH
        )
    source = (exact_dot(tiles[...], weight[...]) + bias[...]).astype(BF)
    slots = devices * per_pair
    chosen = (pick[...] == lax.broadcasted_iota(jnp.int32, (slots, tiles.shape[0]), 1)).astype(BF)
    outbox[...] = exact_dot(chosen, source).reshape(devices, per_pair, width).astype(BF)
    pl.semaphore_wait(barrier, devices - 1)

    order = sorted(range(1, devices), key=lambda k: abs(k - devices // 2))
    first = []
    for k in order:
        peer = (me + k) % devices
        copy = pltpu.make_async_remote_copy(
            src_ref=outbox.at[peer], dst_ref=inbox.at[me], send_sem=send_a.at[k - 1], recv_sem=recv_a.at[k - 1],
            device_id={"seq": peer // tile_n, "tile": peer % tile_n}, device_id_type=MESH,
        )
        copy.start()
        first.append(copy)
    inbox[me] = outbox[me]
    onehot = (own[...] == lax.broadcasted_iota(jnp.int32, (block, 128), 1)).astype(F32)
    row_i = lax.broadcasted_iota(jnp.int32, (block, block), 0)
    col_i = lax.broadcasted_iota(jnp.int32, (block, block), 1)
    before = exact_dot((col_i < row_i).astype(BF), onehot.astype(BF))
    rank = jnp.sum(before * onehot, axis=1, keepdims=True).astype(jnp.int32)
    slot = own[...] * per_pair + rank
    landing = (slot == lax.broadcasted_iota(jnp.int32, (block, slots), 1)).astype(BF)
    span = 1 << levels
    stretch = block // span
    reorder = (reversed_bits(row_i // stretch, levels) + span * (row_i % stretch) == col_i).astype(BF)
    for copy in first:
        copy.wait_recv()
    got = inbox[...].astype(F32).reshape(slots, width).astype(BF)
    embedded = exact_dot(landing, got)
    placed[...] = embedded.astype(BF)
    center = embedded - jnp.mean(embedded, axis=1, keepdims=True)
    spread = jnp.mean(center * center, axis=1, keepdims=True)
    normed = (center * lax.rsqrt(spread + 1e-05) * gain[...] + shift[...]).astype(BF)
    rows[core, 0:block] = exact_dot(reorder, normed).astype(BF)

    second, forwards = [], []
    half = block // 2
    for at, (bit, turn) in enumerate(exchange_plan(levels)):
        count = block >> (bit + 1)
        to = partner(seq, bit, (seq + turn) % (1 << bit))
        start = pl.multiple_of(reversed_bits(to, bit + 1) * count, count)
        land = pl.multiple_of(block + half * bit + (seq % (1 << bit)) * count, count)
        copy = pltpu.make_async_remote_copy(
            src_ref=rows.at[core, pl.ds(start, count)], dst_ref=rows.at[core, pl.ds(land, count)],
            send_sem=send_b.at[at], recv_sem=recv_b.at[at],
            device_id={"seq": to, "tile": core}, device_id_type=MESH,
        )
        copy.start()
        second.append(copy)
    last = len(second)
    copy = pltpu.make_async_remote_copy(
        src_ref=rows.at[core, pl.ds(0, block)], dst_ref=rows.at[core, pl.ds(0, block)],
        send_sem=send_c.at[last], recv_sem=recv_c.at[last],
        device_id={"seq": seq, "tile": other}, device_id_type=MESH,
    )
    copy.start()
    forwards.append(copy)
    for at, (bit, turn) in reversed(list(enumerate(exchange_plan(levels)))):
        count = block >> (bit + 1)
        low = (seq % (1 << bit) + (1 << bit) - turn) % (1 << bit)
        land = pl.multiple_of(block + half * bit + low * count, count)
        second[at].wait_recv()
        copy = pltpu.make_async_remote_copy(
            src_ref=rows.at[core, pl.ds(land, count)], dst_ref=rows.at[core, pl.ds(land, count)],
            send_sem=send_c.at[at], recv_sem=recv_c.at[at],
            device_id={"seq": seq, "tile": other}, device_id_type=MESH,
        )
        copy.start()
        forwards.append(copy)
    for copy in first + second:
        copy.wait_send()
    for copy in forwards:
        copy.wait()


def chunk_list(seq, level, block):
    width = block >> level
    sub = reversed_bits(seq, level) * width
    found = [(sub, seq % (1 << level))]
    for bit in range(level):
        count = block >> (bit + 1)
        inner = sub - reversed_bits(seq, bit + 1) * count
        for low in range(1 << bit):
            found.append(
                (block + (block // 2) * bit + low * count + inner, partner(seq, bit, low) % (1 << level))
            )
    return [(pl.multiple_of(a, width), pl.multiple_of(c * width, width)) for a, c in found]


def attend(levels, slides, dil, ends, rows, weight, bias, back, picked, id_col, id_row, mixed):
    seq = lax.axis_index("seq")
    block = picked.shape[0] // 2
    total = 2 * block
    groups = dil.shape[0]
    group_cols = weight.shape[2] // groups
    head_dim = weight.shape[1] // HEADS
    heads_here = group_cols // head_dim
    factor = math.log2(math.e) / math.sqrt(head_dim)
    span = 1 << levels
    stretch = block // span
    back[...] = jnp.zeros_like(back)

    def slide_of(n, level):
        size = block >> level
        v = n % size
        pos = (
            ((seq >> level) << level) * total + ((n % block) // size) * total + (n // block) * block
            + seq % (1 << level)
            + (reversed_bits(v // stretch, levels - level) << level)
            + span * (v % stretch)
        )
        out = jnp.zeros_like(n)
        for at in range(slides):
            out = out + (pos >= ends[at]).astype(jnp.int32)
        return out

    for g in range(groups):
        offset = g * group_cols // 128 * 128
        wide = -(-(g * group_cols + group_cols - offset) // 128) * 128
        for level in range(levels + 1):
            @pl.when(dil[g] == 1 << level)
            def _():
                size = block >> level
                for side in range(2):
                    for start, put in chunk_list(seq, level, block):
                        picked[pl.ds(side * block + put, size), :] = rows[side, pl.ds(start, size), :]
                id_col[...] = slide_of(lax.broadcasted_iota(jnp.int32, (total, 1), 0), level)
                id_row[...] = slide_of(lax.broadcasted_iota(jnp.int32, (1, total), 1), level)

        x = picked[...]
        triple = [
            (exact_dot(x, weight[m, :, offset : offset + wide]) + bias[m : m + 1, offset : offset + wide]).astype(BF)
            for m in range(3)
        ]
        queries, keys, values = triple
        closed = jnp.where(id_col[...] == id_row[...], 0.0, -1e30)
        lane = lax.broadcasted_iota(jnp.int32, (1, wide), 1)
        result = jnp.zeros((total, wide), F32)
        for h in range(heads_here):
            low = g * group_cols - offset + h * head_dim
            inside = (lane >= low) & (lane < low + head_dim)
            scores = lax.dot_general(
                jnp.where(inside, queries, jnp.zeros((), BF)), keys, (((1,), (1,)), ((), ())),
                preferred_element_type=F32,
            ) + closed
            peak = jnp.max(scores, axis=1, keepdims=True)
            weights = jnp.exp2((scores - peak) * factor)
            norm = jnp.sum(weights, axis=1, keepdims=True)
            result = jnp.where(inside, exact_dot(weights.astype(BF), values) / norm, result)
        mixed[...] = result.astype(BF)
        for level in range(levels + 1):
            @pl.when(dil[g] == 1 << level)
            def _():
                size = block >> level
                for side in range(2):
                    for start, put in chunk_list(seq, level, block):
                        back[side, pl.ds(start, size), offset : offset + wide] += mixed[
                            pl.ds(side * block + put, size), :
                        ]


def give_back(
    levels, local_groups, dil, back, weight, bias, out, arrived, weights, send_a, recv_a, send_b, recv_b
):
    seq, core = lax.axis_index("seq"), lax.axis_index("tile")
    other = 1 - core
    block = out.shape[0]
    half = block // 2
    plan = exchange_plan(levels)
    barrier = pltpu.get_barrier_semaphore()
    peers = []
    for bit, turn in plan:
        to = partner(seq, bit, (seq + turn) % (1 << bit))
        peers += [{"seq": to, "tile": core}, {"seq": to, "tile": other}]
    sibling = {"seq": seq, "tile": other}
    for device in peers + [sibling]:
        pl.semaphore_signal(barrier, inc=1, device_id=device, device_id_type=MESH)
    pl.semaphore_wait(barrier, len(peers) + 1)
    copies = []
    for at, (bit, turn) in enumerate(plan):
        count = block >> (bit + 1)
        low = (seq + turn) % (1 << bit)
        start = pl.multiple_of(block + half * bit + low * count, count)
        land = pl.multiple_of(block + half * bit + (seq % (1 << bit)) * count, count)
        for rel in range(2):
            side = (core + rel) % 2
            copy = pltpu.make_async_remote_copy(
                src_ref=back.at[side, pl.ds(start, count)], dst_ref=arrived.at[core, pl.ds(land, count)],
                send_sem=send_a.at[2 * at + rel], recv_sem=recv_a.at[2 * at + rel],
                device_id={"seq": partner(seq, bit, low), "tile": side}, device_id_type=MESH,
            )
            copy.start()
            copies.append(copy)
    for at, (src, dst) in enumerate(
        [(back.at[other, pl.ds(0, block)], arrived.at[core, pl.ds(0, block)]), (weight, weights.at[core])]
    ):
        copy = pltpu.make_async_remote_copy(
            src_ref=src, dst_ref=dst, send_sem=send_b.at[at], recv_sem=recv_b.at[at],
            device_id=sibling, device_id_type=MESH,
        )
        copy.start()
        copies.append(copy)
    arrived[core, 0:block] = back[core, 0:block]
    weights[core] = weight[...]
    group_cols = weight.shape[0] // local_groups
    span = 1 << levels
    p = lax.broadcasted_iota(jnp.int32, (block, 1), 0)
    home = reversed_bits(p, levels) * (block // span) + p // span
    takes = []
    spots = arrived.shape[1]
    for g in range(2 * local_groups):
        index = home
        for bit in range(levels):
            count = block >> (bit + 1)
            moved = block + half * bit + (p % (1 << bit)) * count + home - reversed_bits(p, bit + 1) * count
            index = jnp.where((bit_of(p, bit) != bit_of(seq, bit)) & (dil[g] > (1 << bit)), moved, index)
        takes.append((index == lax.broadcasted_iota(jnp.int32, (block, spots), 1)).astype(BF))
    for copy in copies:
        copy.wait()
    total = jnp.zeros((block, out.shape[1]), F32) + bias[...]
    for c in range(2):
        for g in range(local_groups):
            offset = g * group_cols // 128 * 128
            wide = -(-(g * group_cols + group_cols - offset) // 128) * 128
            lane = lax.broadcasted_iota(jnp.int32, (1, wide), 1) + offset
            inside = (lane >= g * group_cols) & (lane < (g + 1) * group_cols)
            got = exact_dot(takes[c * local_groups + g], arrived[c, :, offset : offset + wide])
            mine = jnp.where(inside, got, 0.0).astype(BF)
            total = total + exact_dot(mine, weights[c, offset : offset + wide, :])
    out[...] = total.astype(BF)


def on_device(
    tiles, producer, slide_lengths, dilation, in_weight, in_bias, norm_gain, norm_bias,
    qkv_weight, qkv_bias, out_weight, out_bias,
):
    seq_n, tile_n = lax.axis_size("seq"), lax.axis_size("tile")
    devices = seq_n * tile_n
    me = lax.axis_index("seq") * tile_n + lax.axis_index("tile")
    capacity, width = tiles.shape[0], in_weight.shape[1]
    block = producer.shape[0] // devices
    per_pair = capacity // devices
    levels = min(16, seq_n).bit_length() - 1
    spots = block + (block // 2) * levels
    moves = (1 << levels) - 1
    vm = pl.BlockSpec(memory_space=pltpu.VMEM)
    sm = pl.BlockSpec(memory_space=pltpu.SMEM)
    dma = pltpu.SemaphoreType.DMA

    counts = jnp.sum((producer.reshape(devices, block) == me).astype(jnp.int32), axis=1)
    ids = jnp.arange(devices)
    starts = jnp.sum(jnp.where(ids[None, :] < ids[:, None], counts[None, :], 0), axis=1)
    slot = jnp.arange(per_pair, dtype=jnp.int32)
    pick = jnp.where(slot[None, :] < counts[:, None], starts[:, None] + slot[None, :], -1).reshape(-1, 1)
    own = lax.dynamic_slice_in_dim(producer, me * block, block, 0)

    placed, rows = pl.pallas_call(
        functools.partial(hand_over, levels),
        out_shape=(
            jax.ShapeDtypeStruct((block, width), BF),
            jax.ShapeDtypeStruct((tile_n, spots, width), BF),
        ),
        in_specs=[vm] * 7,
        out_specs=(vm, vm),
        scratch_shapes=[
            pltpu.VMEM((devices, per_pair, width), BF),
            pltpu.VMEM((devices, per_pair, width), BF),
            dma((devices - 1,)), dma((devices - 1,)), dma((moves,)), dma((moves,)),
            dma((moves + 1,)), dma((moves + 1,)),
        ],
        compiler_params=pltpu.CompilerParams(
            collective_id=0, has_side_effects=True, vmem_limit_bytes=VMEM_CAP
        ),
    )(
        tiles, in_weight, in_bias.reshape(1, -1), pick, own, norm_gain.reshape(1, -1), norm_bias.reshape(1, -1)
    )

    local_groups = dilation.shape[0] // tile_n
    local_cols = qkv_weight.shape[2]
    wide = -(-(local_cols // local_groups) // 128) * 128
    own_dil = lax.dynamic_slice_in_dim(dilation, lax.axis_index("tile") * local_groups, local_groups)
    back = pl.pallas_call(
        functools.partial(attend, levels, slide_lengths.shape[0]),
        out_shape=jax.ShapeDtypeStruct((tile_n, spots, local_cols), BF),
        in_specs=[sm, sm, vm, vm, vm],
        out_specs=vm,
        scratch_shapes=[
            pltpu.VMEM((2 * block, width), BF),
            pltpu.VMEM((2 * block, 1), jnp.int32),
            pltpu.VMEM((1, 2 * block), jnp.int32),
            pltpu.VMEM((2 * block, wide), BF),
        ],
        compiler_params=pltpu.CompilerParams(vmem_limit_bytes=VMEM_CAP),
    )(own_dil, jnp.cumsum(slide_lengths), rows, qkv_weight, qkv_bias)

    branch = pl.pallas_call(
        functools.partial(give_back, levels, local_groups),
        out_shape=jax.ShapeDtypeStruct((block, width), BF),
        in_specs=[sm, vm, vm, vm],
        out_specs=vm,
        scratch_shapes=[
            pltpu.VMEM((tile_n, spots, local_cols), BF),
            pltpu.VMEM((tile_n,) + out_weight.shape, BF),
            dma((2 * moves,)), dma((2 * moves,)), dma((2,)), dma((2,)),
        ],
        compiler_params=pltpu.CompilerParams(
            collective_id=1, has_side_effects=True, vmem_limit_bytes=VMEM_CAP
        ),
    )(dilation, back, out_weight, out_bias.reshape(1, -1))
    return (placed, branch)


def solution(mesh):
    return jax.shard_map(
        on_device,
        mesh=mesh,
        in_specs=(
            P(("grp", "seq", "tile"), None),
            P("grp", None),
            P("grp"),
            P(),
            P(),
            P(),
            P(),
            P(),
            P(None, None, "tile"),
            P(None, "tile"),
            P("tile", None),
            P(),
        ),
        out_specs=(P(("grp", "seq", "tile"), None), P(("grp", "seq", "tile"), None)),
        check_vma=False,
    )
```

time: 184 us -> 79 us (0.43)
  waiting for transfers between devices: 84 us -> 0 us
  Pallas kernels: 0 us -> 66.4 us
  matrix products: 20.2 us -> 0 us
  local copies, waits for them, and re-layouts: 28.6 us -> 9.98 us
  between operations: 16.1 us -> 0.69 us
  other arithmetic: 17 us -> 1.75 us
  starting transfers between devices: 15.2 us -> 0 us
  blocking collectives: 2.54 us -> 0 us
    pallas_call x0 -> x3, Pallas kernels: none -> 66.4 us  [the longest x1 39.9 us: on_device(): pl.pallas_call(functools.partial(hand_over, levels), out_shape=(jax.Shape...]
    ppermute x6 -> x0, waiting for transfers between devices: 65.4 us -> none  [swapped(): return lax.ppermute(block, axis, route)]
    dot_general x5 -> x0, matrix products: 12.3 us -> none  [the longest x2 5.38 us: segment_attention(): jnp.einsum('hqk,khd->qhd', weights, values, preferred_element_type=jnp.fl...]
    all_to_all x1 -> x0, waiting for transfers between devices: 11.8 us -> none  [on_device(): lax.all_to_all(outgoing, ('seq', 'tile'), split_axis=0, concat_axis=0, ti...]
    sub x2 -> x0, matrix products: 7.9 us -> none  [segment_attention(): exponent = jnp.where(allowed[None], jnp.exp(scores - row_peak), 0.0)]
    ppermute x6 -> x0, starting transfers between devices: 7.82 us -> none  [swapped(): return lax.ppermute(block, axis, route)]
    all_to_all x1 -> x0, starting transfers between devices: 7.39 us -> none  [on_device(): lax.all_to_all(outgoing, ('seq', 'tile'), split_axis=0, concat_axis=0, ti...]
    concatenate x10 -> x0, local copies, waits for them, and re-layouts: 6.85 us -> none  [the longest x1 4.08 us: on_device(): joined_weight = jnp.concatenate(weight_pieces, axis=1)]
  transfers between devices with their start and end apart: 8 -> 0, of which waited for: 8 -> 0; matrix products, arithmetic and copies ran while one was open for 8% -> 0% of each run, Pallas kernels for 0% -> 0%
where the time goes in v1:
time: 79 us; the launch traced here: 78.8 us
  Pallas kernels  66.4 us (84%)
  local copies, waits for them, and re-layouts  9.98 us (13%)
  other arithmetic  1.75 us (2%)
    pallas_call x1, Pallas kernels, on_device(): pl.pallas_call(functools.partial(hand_over, levels), out_shape=(jax.Shape...  39.9 us
    pallas_call x1, Pallas kernels, on_device(): pl.pallas_call(functools.partial(give_back, levels, local_groups), out_sh...  17.1 us
    pallas_call x1, Pallas kernels, on_device(): pl.pallas_call(functools.partial(attend, levels, slide_lengths.shape[0]),...  9.36 us
    unnamed x11, local copies, waits for them, and re-layouts  3.33 us

profile of v1, /device:TPU:0, one launch (start us, length us, event | category | flops | bytes accessed | tf_op | source)
XLA Modules:
  0.0 78.8 jit_solution(1204063097549419698)
XLA Ops:
  0.6 1.3 %reshape.100.bias = f32[1,768]{1,0:T(1,128)} reshape(f32[768]{0:T(1024)} %param.17) | data formatting | bytes 6144 | tf_op jit(solution)/shard_map/reshape | solution.py:336
  1.9 0.8 fusion
  2.7 0.1 reduce_sum.18
  2.8 0.1 select_reduce_fusion
  2.9 0.1 add_select_fusion
  3.0 1.0 %select_n.29.pick = s32[512,1]{1,0:T(8,128)} reshape(s32[16,32]{1,0:T(8,128)S(1)} %add_select_fusion) | data formatting | bytes 4096 | tf_op jit(solution)/shard_map/jit(_where)/select_n | solution.py:315
  4.0 0.7 constant_dynamic-slice_fusion
  4.7 0.8 %copy.19.own = s32[256,1]{1,0:T(8,128)} copy(s32[256,1]{0,1:T(1,128)S(1)} %constant_dynamic-slice_fusion) | data formatting | bytes 2048
  5.5 1.3 %reshape.101.gain = f32[1,768]{1,0:T(1,128)} reshape(f32[768]{0:T(1024)} %param.18) | data formatting | bytes 6144 | tf_op jit(solution)/shard_map/reshape | solution.py:336
  6.7 1.3 %reshape.102.shift = f32[1,768]{1,0:T(1,128)} reshape(f32[768]{0:T(1024)} %param.19) | data formatting | bytes 6144 | tf_op jit(solution)/shard_map/reshape | solution.py:336
  8.0 0.0 copy-start.2
  8.0 0.0 copy-start.3
  8.0 39.9 %shard_map.131 = (bf16[256,768]{1,0:T(8,128)(2,1)}, bf16[2,640,768]{2,1,0:T(8,128)(2,1)}) custom-call(bf16[512,1536]{1,0:T(8,128)(2,1)} %tiles.1, bf16[1536,768]{1,0:T(8,128)(2,1)} %weight.3, f32[1,768]{1,0:T(1,128)} %reshape.100.bias, s32[512,1]{1,0:T(8,128)} %select_n.29.pick, s32[256,1]{1,0:T(8,128)} %copy.19.own, f32[1,768]{1,0:T(1,128)} %reshape.101.gain, ...), custom_call_target="tpu_custom_call" | custom-call | tf_op jit(solution)/shard_map/pallas_call | solution.py:318
  48.0 0.0 copy-done.2
  48.0 0.6 dynamic_slice.7.dil
  48.6 0.0 copy-done.3
  48.6 0.7 reduce-window.9
  49.2 0.0 copy-start.1
  49.2 9.4 %shard_map.132.back = bf16[2,640,384]{2,1,0:T(8,128)(2,1)} custom-call(s32[2]{0:T(128)} %dynamic_slice.7.dil, s32[4]{0:T(128)} %bitcast.2, bf16[2,640,768]{2,1,0:T(8,128)(2,1)} %get-tuple-element.5.rows, bf16[3,768,384]{2,1,0:T(8,128)(2,1)} %weight.4, f32[3,384]{1,0:T(4,128)} %bias.1), custom_call_target="tpu_custom_call" | custom-call | tf_op jit(solution)/shard_map/pallas_call | solution.py:343
  58.6 0.0 copy-done.1
  58.6 0.0 copy-start
  58.6 0.6 reshape.105.bias
  59.2 17.1 %shard_map.133 = bf16[256,768]{1,0:T(8,128)(2,1)} custom-call(s32[4]{0:T(128)} %dil.1, bf16[2,640,384]{2,1,0:T(8,128)(2,1)} %shard_map.132.back, bf16[384,768]{1,0:T(8,128)(2,1)} %weight.5, f32[1,768]{1,0:T(1,128)} %reshape.105.bias), custom_call_target="tpu_custom_call" | custom-call | tf_op jit(solution)/shard_map/pallas_call | solution.py:357
  76.2 0.0 copy-done
  76.3 0.7 copy.22
  77.0 1.8 %copy.23 = bf16[256,768]{1,0:T(8,128)(2,1)} copy(bf16[256,768]{1,0:T(8,128)(2,1)} %shard_map.133) | data formatting | bytes 786432
  (1 shorter events, 0.0 us)
Async XLA Ops:
  8.0 40.0 %copy-start.2 = (s32[4]{0:T(128)S(1)}, s32[4]{0:T(128)}, u32[]{:S(2)}) copy-start(s32[4]{0:T(128)} %dil.1) | copy-start | bytes 52
  8.0 40.6 %copy-start.3 = (s32[4]{0:T(128)S(1)}, s32[4]{0:T(128)}, u32[]{:S(2)}) copy-start(s32[4]{0:T(128)} %param.14) | copy-start | bytes 52
  49.2 9.4 %copy-start.1 = (f32[768]{0:T(1024)S(1)}, f32[768]{0:T(1024)}, u32[]{:S(2)}) copy-start(f32[768]{0:T(1024)} %param.23) | copy-start | bytes 9220
  58.6 17.7 %copy-start = (bf16[256,768]{1,0:T(8,128)(2,1)S(1)}, bf16[256,768]{1,0:T(8,128)(2,1)}, u32[]{:S(2)}) copy-start(bf16[256,768]{1,0:T(8,128)(2,1)} %get-tuple-element.8) | copy-start | bytes 1179652

commit v2 on v1

--- a/solution.py
+++ b/solution.py
@@ -40,7 +40,7 @@
 
 
 def hand_over(
-    levels, tiles, weight, bias, pick, own, gain, shift, placed, rows, outbox, inbox,
+    levels, tiles, weight, bias, owners, gain, shift, placed, rows, outbox, inbox,
     send_a, recv_a, send_b, recv_b, send_c, recv_c,
 ):
     seq_n, tile_n = lax.axis_size("seq"), lax.axis_size("tile")
@@ -49,7 +49,7 @@
     other = 1 - core
     me = seq * tile_n + core
     per_pair = outbox.shape[1]
-    block = own.shape[0]
+    block = owners.shape[2]
     width = outbox.shape[2]
     barrier = pltpu.get_barrier_semaphore()
     for k in range(1, devices):
@@ -57,9 +57,18 @@
         pl.semaphore_signal(
             barrier, inc=1, device_id={"seq": peer // tile_n, "tile": peer % tile_n}, device_id_type=MESH
         )
-    source = (exact_dot(tiles[...], weight[...]) + bias[...]).astype(BF)
+    source = (exact_dot(tiles[...], weight[...]) + bias[...][None, :]).astype(BF)
     slots = devices * per_pair
-    chosen = (pick[...] == lax.broadcasted_iota(jnp.int32, (slots, tiles.shape[0]), 1)).astype(BF)
+    counts = jnp.sum((owners[...] == me).astype(jnp.int32), axis=2, keepdims=True)
+    begin, begins = jnp.zeros((1, 1, 1), jnp.int32), []
+    for at in range(devices):
+        begins.append(begin)
+        begin = begin + counts[at : at + 1]
+    begins = jnp.concatenate(begins, axis=0)
+    cube = (devices, per_pair, tiles.shape[0])
+    nth = lax.broadcasted_iota(jnp.int32, cube, 2) - begins
+    place = lax.broadcasted_iota(jnp.int32, cube, 1)
+    chosen = jnp.where((nth == place) & (place < counts), 1.0, 0.0).reshape(slots, cube[2]).astype(BF)
     outbox[...] = exact_dot(chosen, source).reshape(devices, per_pair, width).astype(BF)
     pl.semaphore_wait(barrier, devices - 1)
 
@@ -74,13 +83,14 @@
         copy.start()
         first.append(copy)
     inbox[me] = outbox[me]
-    onehot = (own[...] == lax.broadcasted_iota(jnp.int32, (block, 128), 1)).astype(F32)
+    own = owners[me]
+    onehot = (own == lax.broadcasted_iota(jnp.int32, (128, block), 0)).astype(F32)
     row_i = lax.broadcasted_iota(jnp.int32, (block, block), 0)
     col_i = lax.broadcasted_iota(jnp.int32, (block, block), 1)
-    before = exact_dot((col_i < row_i).astype(BF), onehot.astype(BF))
-    rank = jnp.sum(before * onehot, axis=1, keepdims=True).astype(jnp.int32)
-    slot = own[...] * per_pair + rank
-    landing = (slot == lax.broadcasted_iota(jnp.int32, (block, slots), 1)).astype(BF)
+    before = exact_dot(onehot.astype(BF), (row_i < col_i).astype(BF))
+    rank = jnp.sum(before * onehot, axis=0, keepdims=True).astype(jnp.int32)
+    slot = own * per_pair + rank
+    landing = (slot == lax.broadcasted_iota(jnp.int32, (slots, block), 0)).astype(F32).T.astype(BF)
     span = 1 << levels
     stretch = block // span
     reorder = (reversed_bits(row_i // stretch, levels) + span * (row_i % stretch) == col_i).astype(BF)
@@ -91,7 +101,7 @@
     placed[...] = embedded.astype(BF)
     center = embedded - jnp.mean(embedded, axis=1, keepdims=True)
     spread = jnp.mean(center * center, axis=1, keepdims=True)
-    normed = (center * lax.rsqrt(spread + 1e-05) * gain[...] + shift[...]).astype(BF)
+    normed = (center * lax.rsqrt(spread + 1e-05) * gain[...][None, :] + shift[...][None, :]).astype(BF)
     rows[core, 0:block] = exact_dot(reorder, normed).astype(BF)
 
     second, forwards = [], []
@@ -148,11 +158,19 @@
     return [(pl.multiple_of(a, width), pl.multiple_of(c * width, width)) for a, c in found]
 
 
-def attend(levels, slides, dil, ends, rows, weight, bias, back, picked, id_col, id_row, mixed):
+def attend(
+    levels, slides, dilation, lengths, rows, weight, bias, embedded, back, kept, picked, id_col, id_row, mixed, sem
+):
+    keep = pltpu.make_async_copy(embedded, kept, sem)
+    keep.start()
     seq = lax.axis_index("seq")
+    ends = [lengths[0]]
+    for at in range(1, slides):
+        ends.append(ends[-1] + lengths[at])
+    groups = dilation.shape[0] // lax.axis_size("tile")
+    dil = [dilation[lax.axis_index("tile") * groups + g] for g in range(groups)]
     block = picked.shape[0] // 2
     total = 2 * block
-    groups = dil.shape[0]
     group_cols = weight.shape[2] // groups
     head_dim = weight.shape[1] // HEADS
     heads_here = group_cols // head_dim
@@ -218,6 +236,7 @@
                         back[side, pl.ds(start, size), offset : offset + wide] += mixed[
                             pl.ds(side * block + put, size), :
                         ]
+    keep.wait()
 
 
 def give_back(
@@ -278,7 +297,7 @@
         takes.append((index == lax.broadcasted_iota(jnp.int32, (block, spots), 1)).astype(BF))
     for copy in copies:
         copy.wait()
-    total = jnp.zeros((block, out.shape[1]), F32) + bias[...]
+    total = jnp.zeros((block, out.shape[1]), F32) + bias[...][None, :]
     for c in range(2):
         for g in range(local_groups):
             offset = g * group_cols // 128 * 128
@@ -297,7 +316,6 @@
 ):
     seq_n, tile_n = lax.axis_size("seq"), lax.axis_size("tile")
     devices = seq_n * tile_n
-    me = lax.axis_index("seq") * tile_n + lax.axis_index("tile")
     capacity, width = tiles.shape[0], in_weight.shape[1]
     block = producer.shape[0] // devices
     per_pair = capacity // devices
@@ -305,15 +323,9 @@
     spots = block + (block // 2) * levels
     moves = (1 << levels) - 1
     vm = pl.BlockSpec(memory_space=pltpu.VMEM)
+    hbm = pl.BlockSpec(memory_space=pl.ANY)
     sm = pl.BlockSpec(memory_space=pltpu.SMEM)
     dma = pltpu.SemaphoreType.DMA
-
-    counts = jnp.sum((producer.reshape(devices, block) == me).astype(jnp.int32), axis=1)
-    ids = jnp.arange(devices)
-    starts = jnp.sum(jnp.where(ids[None, :] < ids[:, None], counts[None, :], 0), axis=1)
-    slot = jnp.arange(per_pair, dtype=jnp.int32)
-    pick = jnp.where(slot[None, :] < counts[:, None], starts[:, None] + slot[None, :], -1).reshape(-1, 1)
-    own = lax.dynamic_slice_in_dim(producer, me * block, block, 0)
 
     placed, rows = pl.pallas_call(
         functools.partial(hand_over, levels),
@@ -321,7 +333,7 @@
             jax.ShapeDtypeStruct((block, width), BF),
             jax.ShapeDtypeStruct((tile_n, spots, width), BF),
         ),
-        in_specs=[vm] * 7,
+        in_specs=[vm] * 6,
         out_specs=(vm, vm),
         scratch_shapes=[
             pltpu.VMEM((devices, per_pair, width), BF),
@@ -333,26 +345,29 @@
             collective_id=0, has_side_effects=True, vmem_limit_bytes=VMEM_CAP
         ),
     )(
-        tiles, in_weight, in_bias.reshape(1, -1), pick, own, norm_gain.reshape(1, -1), norm_bias.reshape(1, -1)
+        tiles, in_weight, in_bias, producer.reshape(devices, 1, block), norm_gain, norm_bias
     )
 
     local_groups = dilation.shape[0] // tile_n
     local_cols = qkv_weight.shape[2]
     wide = -(-(local_cols // local_groups) // 128) * 128
-    own_dil = lax.dynamic_slice_in_dim(dilation, lax.axis_index("tile") * local_groups, local_groups)
-    back = pl.pallas_call(
+    back, kept = pl.pallas_call(
         functools.partial(attend, levels, slide_lengths.shape[0]),
-        out_shape=jax.ShapeDtypeStruct((tile_n, spots, local_cols), BF),
-        in_specs=[sm, sm, vm, vm, vm],
-        out_specs=vm,
+        out_shape=(
+            jax.ShapeDtypeStruct((tile_n, spots, local_cols), BF),
+            jax.ShapeDtypeStruct((block, width), BF),
+        ),
+        in_specs=[sm, sm, vm, vm, vm, hbm],
+        out_specs=(vm, hbm),
         scratch_shapes=[
             pltpu.VMEM((2 * block, width), BF),
             pltpu.VMEM((2 * block, 1), jnp.int32),
             pltpu.VMEM((1, 2 * block), jnp.int32),
             pltpu.VMEM((2 * block, wide), BF),
+            dma,
         ],
         compiler_params=pltpu.CompilerParams(vmem_limit_bytes=VMEM_CAP),
-    )(own_dil, jnp.cumsum(slide_lengths), rows, qkv_weight, qkv_bias)
+    )(dilation, slide_lengths, rows, qkv_weight, qkv_bias, placed)
 
     branch = pl.pallas_call(
         functools.partial(give_back, levels, local_groups),
@@ -367,8 +382,8 @@
         compiler_params=pltpu.CompilerParams(
             collective_id=1, has_side_effects=True, vmem_limit_bytes=VMEM_CAP
         ),
-    )(dilation, back, out_weight, out_bias.reshape(1, -1))
-    return (placed, branch)
+    )(dilation, back, out_weight, out_bias)
+    return (kept, branch)
 
 
 def solution(mesh):

time: 79 us -> 75.7 us (0.958)
  local copies, waits for them, and re-layouts: 9.98 us -> 1.77 us
  Pallas kernels: 66.4 us -> 73.1 us
  other arithmetic: 1.75 us -> 0 us
    pallas_call x1, Pallas kernels: 9.36 us -> 16.1 us  [on_device(): pl.pallas_call(functools.partial(attend, levels, slide_lengths.shape[0]),...]
    reshape x4 -> x0, local copies, waits for them, and re-layouts: 4.4 us -> none  [the longest x1 1.28 us: on_device(): in_bias.reshape(1, -1)]
    unnamed x11 -> x1, local copies, waits for them, and re-layouts: 3.33 us -> 1.77 us
    dynamic_slice x2 -> x0, local copies, waits for them, and re-layouts: 1.27 us -> none  [the longest x1 0.68 us: on_device(): own = lax.dynamic_slice_in_dim(producer, me * block, block, 0)]
    select_n x1 -> x0, local copies, waits for them, and re-layouts: 0.97 us -> none  [on_device(): jnp.where(slot[None, :] < counts[:, None], starts[:, None] + slot[None, :...]
where the time goes in v2:
time: 75.7 us; the launch traced here: 75.5 us
  Pallas kernels  73.1 us (97%)
  local copies, waits for them, and re-layouts  1.77 us (2%)
    pallas_call x1, Pallas kernels, on_device(): pl.pallas_call(functools.partial(hand_over, levels), out_shape=(jax.Shape...  39.9 us
    pallas_call x1, Pallas kernels, on_device(): pl.pallas_call(functools.partial(give_back, levels, local_groups), out_sh...  17.1 us
    pallas_call x1, Pallas kernels, on_device(): pl.pallas_call(functools.partial(attend, levels, slide_lengths.shape[0]),...  16.1 us
    unnamed x1, local copies, waits for them, and re-layouts  1.77 us

profile of v2, /device:TPU:0, one launch (start us, length us, event | category | flops | bytes accessed | tf_op | source)
XLA Modules:
  0.0 75.5 jit_solution(8144792773285429482)
XLA Ops:
  0.6 39.9 %shard_map.131 = (bf16[256,768]{1,0:T(8,128)(2,1)}, bf16[2,640,768]{2,1,0:T(8,128)(2,1)}) custom-call(bf16[512,1536]{1,0:T(8,128)(2,1)} %tiles.1, bf16[1536,768]{1,0:T(8,128)(2,1)} %weight.3, f32[768]{0:T(1024)} %bias.3, s32[16,1,256]{2,1,0:T(1,128)} %bitcast.1, f32[768]{0:T(1024)} %gain.1, f32[768]{0:T(1024)} %shift.1), custom_call_target="tpu_custom_call" | custom-call | tf_op jit(solution)/shard_map/pallas_call | solution.py:330
  40.6 16.1 %shard_map.132 = (bf16[2,640,384]{2,1,0:T(8,128)(2,1)}, bf16[256,768]{1,0:T(8,128)(2,1)}) custom-call(s32[4]{0:T(128)} %dil.1, s32[4]{0:T(128)} %lengths.1, bf16[2,640,768]{2,1,0:T(8,128)(2,1)} %get-tuple-element.6.rows, bf16[3,768,384]{2,1,0:T(8,128)(2,1)} %weight.4, f32[3,384]{1,0:T(4,128)} %bias.4, bf16[256,768]{1,0:T(8,128)(2,1)} %get-tuple-element.7.embedded), custom_call_target="tpu_custom_call" | custom-call | tf_op jit(solution)/shard_map/pallas_call | solution.py:354
  56.6 17.1 %shard_map.133 = bf16[256,768]{1,0:T(8,128)(2,1)} custom-call(s32[4]{0:T(128)} %dil.1, bf16[2,640,384]{2,1,0:T(8,128)(2,1)} %get-tuple-element.9.back, bf16[384,768]{1,0:T(8,128)(2,1)} %weight.5, f32[768]{0:T(1024)} %bias.5), custom_call_target="tpu_custom_call" | custom-call | tf_op jit(solution)/shard_map/pallas_call | solution.py:372
  73.7 1.8 %copy.15 = bf16[256,768]{1,0:T(8,128)(2,1)} copy(bf16[256,768]{1,0:T(8,128)(2,1)} %shard_map.133) | data formatting | bytes 786432

commit v3 on v2

--- a/solution.py
+++ b/solution.py
@@ -358,7 +358,7 @@
             jax.ShapeDtypeStruct((block, width), BF),
         ),
         in_specs=[sm, sm, vm, vm, vm, hbm],
-        out_specs=(vm, hbm),
+        out_specs=(vm, vm),
         scratch_shapes=[
             pltpu.VMEM((2 * block, width), BF),
             pltpu.VMEM((2 * block, 1), jnp.int32),

time: 75.7 us -> 68.9 us (0.910)
  Pallas kernels: 73.1 us -> 66.2 us
    pallas_call x1, Pallas kernels: 16.1 us -> 9.24 us  [on_device(): pl.pallas_call(functools.partial(attend, levels, slide_lengths.shape[0]),...]
where the time goes in v3:
time: 68.9 us; the launch traced here: 68.7 us
  Pallas kernels  66.2 us (96%)
  local copies, waits for them, and re-layouts  1.77 us (3%)
    pallas_call x1, Pallas kernels, on_device(): pl.pallas_call(functools.partial(hand_over, levels), out_shape=(jax.Shape...  39.9 us
    pallas_call x1, Pallas kernels, on_device(): pl.pallas_call(functools.partial(give_back, levels, local_groups), out_sh...  17.1 us
    pallas_call x1, Pallas kernels, on_device(): pl.pallas_call(functools.partial(attend, levels, slide_lengths.shape[0]),...  9.24 us
    unnamed x1, local copies, waits for them, and re-layouts  1.77 us

profile of v3, /device:TPU:0, one launch (start us, length us, event | category | flops | bytes accessed | tf_op | source)
XLA Modules:
  0.0 68.7 jit_solution(16825388004122309602)
XLA Ops:
  0.6 39.9 %shard_map.131 = (bf16[256,768]{1,0:T(8,128)(2,1)}, bf16[2,640,768]{2,1,0:T(8,128)(2,1)}) custom-call(bf16[512,1536]{1,0:T(8,128)(2,1)} %tiles.1, bf16[1536,768]{1,0:T(8,128)(2,1)} %weight.3, f32[768]{0:T(1024)} %bias.3, s32[16,1,256]{2,1,0:T(1,128)} %bitcast.1, f32[768]{0:T(1024)} %gain.1, f32[768]{0:T(1024)} %shift.1), custom_call_target="tpu_custom_call" | custom-call | tf_op jit(solution)/shard_map/pallas_call | solution.py:330
  40.6 9.2 %shard_map.132 = (bf16[2,640,384]{2,1,0:T(8,128)(2,1)}, bf16[256,768]{1,0:T(8,128)(2,1)}) custom-call(s32[4]{0:T(128)} %dil.1, s32[4]{0:T(128)} %lengths.1, bf16[2,640,768]{2,1,0:T(8,128)(2,1)} %get-tuple-element.6.rows, bf16[3,768,384]{2,1,0:T(8,128)(2,1)} %weight.4, f32[3,384]{1,0:T(4,128)} %bias.4, bf16[256,768]{1,0:T(8,128)(2,1)} %get-tuple-element.7.embedded), custom_call_target="tpu_custom_call" | custom-call | tf_op jit(solution)/shard_map/pallas_call | solution.py:354
  49.8 17.1 %shard_map.133 = bf16[256,768]{1,0:T(8,128)(2,1)} custom-call(s32[4]{0:T(128)} %dil.1, bf16[2,640,384]{2,1,0:T(8,128)(2,1)} %get-tuple-element.9.back, bf16[384,768]{1,0:T(8,128)(2,1)} %weight.5, f32[768]{0:T(1024)} %bias.5), custom_call_target="tpu_custom_call" | custom-call | tf_op jit(solution)/shard_map/pallas_call | solution.py:372
  66.9 1.8 %copy.15 = bf16[256,768]{1,0:T(8,128)(2,1)} copy(bf16[256,768]{1,0:T(8,128)(2,1)} %shard_map.133) | data formatting | bytes 786432
